TPU v7x, 256 devices: a whole 4x4x8 slice. The times are simulated.
256 devices in a mesh: batch: 16 (over z_hi, x, core), patch: 16 (over y, z_lo).
Axes of the slice: x: 4, y: 4, z: 8 (z_hi: 2, z_lo: 4; z = z_hi * 4 + z_lo), core: 2. Of those that a mesh axis runs over, the one named last changes fastest.
Arguments:
- latent: bfloat16 [512, 64, 1280], P(('batch', 'patch')), parts along dimension 0, may hold values from -100 to 100
- conv_weight: bfloat16 [3, 3, 1280, 1280], P(None, None, 'patch'), may hold values from -0.25 to 0.25
- channel_bias: float32 [1280], P('patch'), may hold values from -6 to 6
- w_query: bfloat16 [1280, 1280], P('patch'), may hold values from -0.5 to 0.5
- w_key: bfloat16 [1280, 1280], P('patch'), may hold values from -0.5 to 0.5
- w_value: bfloat16 [1280, 1280], P('patch'), may hold values from -0.15625 to 0.15625
- w_out: bfloat16 [1280, 1280], P('patch'), may hold values from -0.15625 to 0.15625
Outputs:
- output: bfloat16 [512, 64, 1280], P(('batch', 'patch')), parts along dimension 0
There are 16 independent parts, one for each index of `batch`. A program takes and returns all parts, laid end to end along the dimension named above; an argument that names none is the same for every part. Nothing has to cross between parts.
All inputs are finite; a program needn't handle non-finite values.
Results may differ from a plain program's by a relative error of at most 0.015.
Values may be sent and summed in bfloat16 or wider, within the bound.
A program may use at most 128 MiB of HBM per device.

v0:
```python
import jax
import jax.numpy as jnp
from jax import lax
from jax.sharding import PartitionSpec as P

C = 1280
HEADS = 20
HEAD_DIM = 64
GROUPS = 32
epsilon = 1e-05


def contract(left, right):
    return lax.dot_general(
        left, right, (((1,), (1,)), ((), ())), preferred_element_type=jnp.float32
    )


def group_norm(values, entries):
    grouped = values.reshape(-1, GROUPS, C // GROUPS)
    centre = lax.psum(jnp.sum(grouped, axis=(0, 2)), "patch") / entries
    deviation = grouped - centre[None, :, None]
    spread = lax.psum(jnp.sum(jnp.square(deviation), axis=(0, 2)), "patch") / entries
    normalized = (grouped - centre[None, :, None]) * lax.rsqrt(spread + epsilon)[None, :, None]
    return normalized.reshape(values.shape)


def convolve(padded, kernel, row_count, columns):
    running = jnp.zeros((row_count * columns, kernel.shape[2]), jnp.float32)
    for row_shift in range(3):
        for col_shift in range(3):
            window = padded[
                row_shift : row_shift + row_count, col_shift : col_shift + columns, :
            ].reshape(-1, C)
            running = running + contract(window, kernel[row_shift, col_shift])
    return running


def attend(queries, key_all, value_all):
    query_heads = queries.reshape(-1, HEADS, HEAD_DIM).transpose(1, 0, 2)
    key_heads = key_all.reshape(-1, HEADS, HEAD_DIM).transpose(1, 0, 2)
    value_heads = value_all.reshape(-1, HEADS, HEAD_DIM).transpose(1, 0, 2)

    def one_head(triple):
        query_one, key_one, value_one = triple
        scores = jnp.dot(query_one, key_one.T, preferred_element_type=jnp.float32) * HEAD_DIM ** (
            -0.5
        )
        row_peak = jnp.max(scores, axis=1, keepdims=True)
        unnormalized = jnp.exp(scores - row_peak)
        row_total = jnp.sum(unnormalized, axis=1, keepdims=True)
        mixture = jnp.dot(
            unnormalized.astype(jnp.bfloat16), value_one, preferred_element_type=jnp.float32
        )
        return mixture / row_total

    heads_out = lax.map(one_head, (query_heads, key_heads, value_heads))
    return heads_out.transpose(1, 0, 2).reshape(-1, C).astype(jnp.bfloat16)


def on_device(latent, conv_weight, channel_bias, w_query, w_key, w_value, w_out):
    rows_local, columns, channels = latent.shape
    devices = lax.axis_size("patch")
    entries = rows_local * devices * columns * (channels // GROUPS)
    inputs = latent.astype(jnp.float32)
    activated = jax.nn.silu(group_norm(inputs, entries)).astype(jnp.bfloat16)
    whole_image = lax.all_gather(activated, "patch", axis=0, tiled=True)
    all_rows = whole_image.shape[0]
    padded = jnp.pad(whole_image, ((1, 1), (1, 1), (0, 0)))
    convolved = convolve(padded, conv_weight, all_rows, columns) + channel_bias
    convolved = convolved.reshape(all_rows, columns, -1)
    returned = lax.all_to_all(
        convolved.astype(jnp.bfloat16), "patch", split_axis=0, concat_axis=2, tiled=True
    ).astype(convolved.dtype)
    hidden = (inputs + returned).astype(jnp.bfloat16)
    hidden = lax.optimization_barrier(hidden)
    residual = hidden.astype(jnp.float32).reshape(-1, channels)
    normed = group_norm(residual, entries).astype(jnp.bfloat16)
    full_query, full_key, full_value = (
        lax.all_gather(w_query, "patch", axis=0, tiled=True),
        lax.all_gather(w_key, "patch", axis=0, tiled=True),
        lax.all_gather(w_value, "patch", axis=0, tiled=True),
    )
    queries = contract(normed, full_query).astype(jnp.bfloat16)
    key_local = contract(normed, full_key).astype(jnp.bfloat16)
    value_local = contract(normed, full_value).astype(jnp.bfloat16)
    key_all, value_all = (
        lax.all_gather(key_local, "patch", axis=0, tiled=True),
        lax.all_gather(value_local, "patch", axis=0, tiled=True),
    )
    attended = attend(queries, key_all, value_all)
    projected = contract(attended, lax.all_gather(w_out, "patch", axis=0, tiled=True))
    output = (residual + projected).astype(jnp.bfloat16)
    return output.reshape(rows_local, columns, channels)


def solution(mesh):
    return jax.shard_map(
        on_device,
        mesh=mesh,
        in_specs=(
            P(("batch", "patch"), None, None),
            P(None, None, "patch", None),
            P("patch"),
            P("patch", None),
            P("patch", None),
            P("patch", None),
            P("patch", None),
        ),
        out_specs=P(("batch", "patch"), None, None),
        check_vma=False,
    )
```

profile of v0, /device:TPU:2, one launch (start us, length us, event | category | flops | bytes accessed | tf_op | source)
XLA Modules:
  0.0 847.6 jit_solution(9786328990870894424)
XLA Ops:
  7.8 45.0 %psum.28 = f32[32]{0:T(128)S(1)} all-reduce(f32[32]{0:T(128)S(1)} %reduce_sum.59), channel_id=1, replica_groups=mesh['batch'=16,'patch'=16] {'patch'}, use_global_device_ids=true, to_apply=%region_2.0 | all-reduce | flops 32 | bytes 256 | tf_op jit(solution)/shard_map/psum | solution.py:21
  54.3 38.0 %psum.29 = f32[32]{0:T(128)S(1)} all-reduce(f32[32]{0:T(128)S(1)} %reduce_sum.62), channel_id=1, replica_groups=mesh['batch'=16,'patch'=16] {'patch'}, use_global_device_ids=true, to_apply=%region_5.6 | all-reduce | flops 32 | bytes 256 | tf_op jit(solution)/shard_map/psum | solution.py:23
  92.4 1.9 fusion.24
  96.5 119.0 %all-gather.8.cloned.1.call-done = bf16[32,64,1280]{2,1,0:T(8,128)(2,1)} async-done(((bf16[2,64,1280]{2,1,0:T(8,128)(2,1)}), bf16[32,64,1280]{2,1,0:T(8,128)(2,1)}) %all-gather.8.cloned.1.call-update) | async-done | bytes 5242896 | tf_op jit(solution)/shard_map/all_gather | solution.py:67
  215.5 31.0 %pad_slice_fusion = (bf16[32,64,1280]{2,1,0:T(8,128)(2,1)S(1)}, bf16[32,64,1280]{2,1,0:T(8,128)(2,1)}, bf16[32,64,1280]{2,1,0:T(8,128)(2,1)}, bf16[32,64,1280]{2...) fusion(bf16[32,64,1280]{2,1,0:T(8,128)(2,1)} %all-gather.8.clon, ...), kind=kLoop, calls=%fused_computation.16 | loop fusion | bytes 47185920 | tf_op jit(solution)/shard_map/slice | solution.py:32
  246.6 4.3 fusion.37
  251.0 1.7 convolution_add_fusion.8
  253.5 1.7 convolution_add_fusion.7
  255.2 1.7 convolution_add_fusion.6
  257.4 1.7 convolution_add_fusion.5
  259.1 1.7 convolution_add_fusion.4
  260.8 1.7 convolution_add_fusion.3
  262.6 1.7 convolution_add_fusion.2
  264.3 1.7 fusion.16
  266.3 33.4 %all_to_all.4 = bf16[32,64,80]{2,1,0:T(8,128)(2,1)S(1)} all-to-all(bf16[32,64,80]{2,1,0:T(8,128)(2,1)S(1)} %bitcast.133), channel_id=1, replica_groups=mesh['batch'=16,'patch'=16] {'patch'}, dimensions={0} | all-to-all | bytes 655360 | tf_op jit(solution)/shard_map/all_to_all | solution.py:72
  300.8 38.8 %psum.30 = f32[32]{0:T(128)S(1)} all-reduce(f32[32]{0:T(128)S(1)} %reduce_sum.81), channel_id=1, replica_groups=mesh['batch'=16,'patch'=16] {'patch'}, use_global_device_ids=true, to_apply=%region_8.9 | all-reduce | flops 32 | bytes 256 | tf_op jit(solution)/shard_map/psum | solution.py:21
  340.1 40.1 %psum.31 = f32[32]{0:T(128)S(1)} all-reduce(f32[32]{0:T(128)S(1)} %reduce_sum.84), channel_id=1, replica_groups=mesh['batch'=16,'patch'=16] {'patch'}, use_global_device_ids=true, to_apply=%region_11.12 | all-reduce | flops 32 | bytes 256 | tf_op jit(solution)/shard_map/psum | solution.py:23
  380.5 3.9 convolution_convert_fusion.1
  384.4 23.6 %all-gather.16.cloned.1.call-done = bf16[1280,1280]{1,0:T(8,128)(2,1)} async-done(((bf16[80,1280]{1,0:T(8,128)(2,1)}), bf16[1280,1280]{1,0:T(8,128)(2,1)}) %all-gather.16.cloned.1.call-update) | async-done | bytes 3276816 | tf_op jit(solution)/shard_map/all_gather | solution.py:82
  408.0 3.8 convolution_convert_fusion
  412.6 86.3 %all-gather.10.cloned.1.call-done = bf16[1280,1280]{1,0:T(8,128)(2,1)} async-done(((bf16[80,1280]{1,0:T(8,128)(2,1)}), bf16[1280,1280]{1,0:T(8,128)(2,1)}) %all-gather.10.cloned.1.call-update) | async-done | bytes 3276816 | tf_op jit(solution)/shard_map/all_gather | solution.py:80
  499.0 3.1 convolution_convert_fusion.2
  502.3 118.9 %all-gather.14.cloned.1.call-done = bf16[2048,1280]{1,0:T(8,128)(2,1)} async-done(((bf16[128,1280]{1,0:T(8,128)(2,1)}), bf16[2048,1280]{1,0:T(8,128)(2,1)}) %all-gather.14.cloned.1.call-update) | async-done | bytes 5242896 | tf_op jit(solution)/shard_map/all_gather | solution.py:88
  621.2 7.9 copy.30
  629.1 114.0 %all-gather.18.cloned.1.call-done = bf16[2048,1280]{1,0:T(8,128)(2,1)} async-done(((bf16[128,1280]{1,0:T(8,128)(2,1)}), bf16[2048,1280]{1,0:T(8,128)(2,1)}) %all-gather.18.cloned.1.call-update) | async-done | bytes 5242896 | tf_op jit(solution)/shard_map/all_gather | solution.py:89
  743.1 8.0 copy.31
  751.1 60.3 %while.10 = (s32[]{:T(128)}, bf16[20,128,64]{1,2,0:T(8,128)(2,1)S(1)}, bf16[20,128,64]{1,2,0:T(8,128)(2,1)S(1)}, bf16[20,2048,64]{1,2,0:T(8,128)(2,1)}, bf16[20,2048,64]{1,2,0:T(8,128)(2,1)}, /*index=5*/s32[]{:T(128)}) while((s32[]{:T(128)}, bf16[20,128,64]{1,2,0:T(8,128)(2,1)S(1)}, bf16[20,128,64]{1,2,0:T(8,128)(2,1)S(1)}, ...), condition=%wide.region_15.16_spmd, body=%wide.region_12.15_spmd.sunk | while | flops 68689664 | bytes 3723845 | solution.py:57
  778.3 1.4 fusion.73
  793.3 1.4 fusion.73
  805.4 1.4 fusion.73
  811.5 25.4 %all-gather.20.cloned.1.call-done = bf16[1280,1280]{1,0:T(8,128)(2,1)} async-done(((bf16[80,1280]{1,0:T(8,128)(2,1)}), bf16[1280,1280]{1,0:T(8,128)(2,1)}) %all-gather.20.cloned.1.call-update) | async-done | bytes 3276816 | tf_op jit(solution)/shard_map/all_gather | solution.py:92
  836.9 3.9 fusion.14
  (138 shorter events, 65.2 us)
Async XLA Ops:
  6.5 209.0 %all-gather.8.cloned.1.call-start = ((), (), s32[]{:S(2)}) async-start(), calls=%async_computation.1 | async-start | bytes 5570560 | tf_op jit(solution)/shard_map/all_gather | solution.py:67
  94.4 286.1 %all-gather.12.cloned.1.call-start = ((), (), s32[]{:S(2)}) async-start(), calls=%async_computation.3 | async-start | bytes 3481600 | tf_op jit(solution)/shard_map/all_gather | solution.py:81
  95.1 312.9 %all-gather.16.cloned.1.call-start = ((), (), s32[]{:S(2)}) async-start(), calls=%async_computation.5 | async-start | bytes 3481600 | tf_op jit(solution)/shard_map/all_gather | solution.py:82
  95.8 403.1 %all-gather.10.cloned.1.call-start = ((), (), s32[]{:S(2)}) async-start(), calls=%async_computation.2 | async-start | bytes 3481600 | tf_op jit(solution)/shard_map/all_gather | solution.py:80
  96.4 150.2 %copy-start.3 = (bf16[3,3,80,1280]{3,2,1,0:T(8,128)(2,1)S(1)}, bf16[3,3,80,1280]{3,2,1,0:T(8,128)(2,1)}, u32[]{:S(2)}) copy-start(bf16[3,3,80,1280]{3,2,1,0:T(8,128)(2,1)} %param.10) | copy-start | bytes 5529604
  96.4 524.7 %all-gather.14.cloned.1.call-start = ((), (), s32[]{:S(2)}) async-start(), calls=%async_computation.4 | async-start | bytes 5570560 | tf_op jit(solution)/shard_map/all_gather | solution.py:88
  246.6 4.4 copy-start.1
  246.6 8.6 %slice-start.8 = ((s8[5242880]{0:T(1024)(128)(4,1)}), s8[4194304]{0:T(1024)(128)(4,1)S(1)}, s32[]{:S(2)}) async-start(s8[5242880]{0:T(1024)(128)(4,1)} %bitcast.122), calls=%async_computation.16 | async-start | bytes 8388608
  250.9 2.5 copy-start
  251.0 4.2 slice-start.9
  253.5 3.5 slice-start
  253.5 5.6 slice-start.6
  255.2 2.2 slice-start.1
  255.2 3.9 slice-start.7
  256.9 3.9 slice-start.4
  259.1 1.8 slice-start.5
  259.1 3.5 slice-start.2
  260.8 1.7 slice-start.3
  262.5 1.7 copy-start.4
  264.3 36.2 %copy-start.2 = (bf16[2,64,1280]{2,1,0:T(8,128)(2,1)S(1)}, bf16[2,64,1280]{2,1,0:T(8,128)(2,1)}, u32[]{:S(2)}) copy-start(bf16[2,64,1280]{2,1,0:T(8,128)(2,1)} %param.9) | copy-start | bytes 983044
  384.3 358.8 %all-gather.18.cloned.1.call-start = ((), (), s32[]{:S(2)}) async-start(), calls=%async_computation.6 | async-start | bytes 5570560 | tf_op jit(solution)/shard_map/all_gather | solution.py:89
  411.9 425.0 %all-gather.20.cloned.1.call-start = ((), (), s32[]{:S(2)}) async-start(), calls=%async_computation.7 | async-start | bytes 3481600 | tf_op jit(solution)/shard_map/all_gather | solution.py:92
Sparse Core Ops, SparseCore 0:
  94.5 120.9 all-gather.7
  217.3 97.4 all-gather.11
  316.6 91.3 all-gather.15
  409.7 89.2 all-gather.9
  500.6 120.5 all-gather.13
  622.8 120.2 all-gather.17
  744.9 91.8 all-gather.19
where the time goes:
time: 850 us; the launch traced here: 848 us
  waiting for transfers between devices  490 us (58%)
  blocking collectives  195 us (23%)
  matrix products  86.4 us (10%)
  local copies, waits for them, and re-layouts  50.5 us (6%)
  between operations  13.9 us (2%)
  other arithmetic  10.9 us (1%)
    all_gather x1, waiting for transfers between devices, on_device(): whole_image = lax.all_gather(activated, 'patch', axis=0, tiled=True)  119 us
    all_gather x1, waiting for transfers between devices, on_device(): lax.all_gather(key_local, 'patch', axis=0, tiled=True)  119 us
    all_gather x1, waiting for transfers between devices, on_device(): lax.all_gather(value_local, 'patch', axis=0, tiled=True)  114 us
    all_gather x1, waiting for transfers between devices, on_device(): lax.all_gather(w_query, 'patch', axis=0, tiled=True)  86.3 us
    psum x2, blocking collectives, group_norm(): centre = lax.psum(jnp.sum(grouped, axis=(0, 2)), 'patch') / entries  83.8 us
    psum x2, blocking collectives, group_norm(): lax.psum(jnp.sum(jnp.square(deviation), axis=(0, 2)), 'patch') / entries  78.1 us
    all_to_all x1, blocking collectives, on_device(): lax.all_to_all(convolved.astype(jnp.bfloat16), 'patch', split_axis=0, con...  33.4 us
    dot_general x13, matrix products, contract(): lax.dot_general(left, right, (((1,), (1,)), ((), ())), preferred_element_...  32.6 us
  transfers between devices with their start and end apart: 7, of which 6 were waited for; matrix products, arithmetic and copies ran while one was open for 16% of the time, Pallas kernels for 0%

commit v1 on v0

--- a/solution.py
+++ b/solution.py
@@ -89,7 +89,12 @@
         lax.all_gather(value_local, "patch", axis=0, tiled=True),
     )
     attended = attend(queries, key_all, value_all)
-    projected = contract(attended, lax.all_gather(w_out, "patch", axis=0, tiled=True))
+    projected = contract(
+        attended,
+        jnp.concatenate(
+            lax.all_to_all(jnp.stack([w_out] * lax.axis_size("patch")), "patch", 0, 0), axis=0
+        ),
+    )
     output = (residual + projected).astype(jnp.bfloat16)
     return output.reshape(rows_local, columns, channels)
 

time: 850 us -> 887 us (1.044)
  waiting for transfers between devices: 490 us -> 507 us
  matrix products: 86.4 us -> 98.7 us
    all_gather x1, waiting for transfers between devices: 86.3 us -> 131 us  [on_device(): lax.all_gather(w_query, 'patch', axis=0, tiled=True)]
    all_gather x1 -> x0, waiting for transfers between devices: 25.4 us -> none  [on_device(): lax.all_gather(w_out, 'patch', axis=0, tiled=True)]
    dot_general x20, matrix products: 26.8 us -> 38.7 us  [one_head(): jnp.dot(unnormalized.astype(jnp.bfloat16), value_one, preferred_element_t...]
  transfers between devices with their start and end apart: 7 -> 7, of which waited for: 6 -> 5; matrix products, arithmetic and copies ran while one was open for 16% -> 17% of each run, Pallas kernels for 0% -> 0%
where the time goes in v1:
time: 887 us; the launch traced here: 884 us
  waiting for transfers between devices  507 us (57%)
  blocking collectives  195 us (22%)
  matrix products  98.7 us (11%)
  local copies, waits for them, and re-layouts  54.1 us (6%)
  between operations  13.9 us (2%)
  other arithmetic  10.9 us (1%)
    all_gather x1, waiting for transfers between devices, on_device(): lax.all_gather(w_query, 'patch', axis=0, tiled=True)  131 us
    all_gather x1, waiting for transfers between devices, on_device(): whole_image = lax.all_gather(activated, 'patch', axis=0, tiled=True)  119 us
    all_gather x1, waiting for transfers between devices, on_device(): lax.all_gather(key_local, 'patch', axis=0, tiled=True)  117 us
    all_gather x1, waiting for transfers between devices, on_device(): lax.all_gather(value_local, 'patch', axis=0, tiled=True)  114 us
    psum x2, blocking collectives, group_norm(): centre = lax.psum(jnp.sum(grouped, axis=(0, 2)), 'patch') / entries  83.9 us
    psum x2, blocking collectives, group_norm(): lax.psum(jnp.sum(jnp.square(deviation), axis=(0, 2)), 'patch') / entries  77.7 us
    dot_general x20, matrix products, one_head(): jnp.dot(unnormalized.astype(jnp.bfloat16), value_one, preferred_element_t...  38.7 us
    all_to_all x1, blocking collectives, on_device(): lax.all_to_all(convolved.astype(jnp.bfloat16), 'patch', split_axis=0, con...  33.3 us
  transfers between devices with their start and end apart: 7, of which 5 were waited for; matrix products, arithmetic and copies ran while one was open for 17% of the time, Pallas kernels for 0%

profile of v1, /device:TPU:2, one launch (start us, length us, event | category | flops | bytes accessed | tf_op | source)
XLA Modules:
  0.0 884.4 jit_solution(15941524504817885151)
XLA Ops:
  7.8 45.0 %psum.28 = f32[32]{0:T(128)S(1)} all-reduce(f32[32]{0:T(128)S(1)} %reduce_sum.59), channel_id=1, replica_groups=mesh['batch'=16,'patch'=16] {'patch'}, use_global_device_ids=true, to_apply=%region_2.0 | all-reduce | flops 32 | bytes 256 | tf_op jit(solution)/shard_map/psum | solution.py:21
  54.3 38.0 %psum.29 = f32[32]{0:T(128)S(1)} all-reduce(f32[32]{0:T(128)S(1)} %reduce_sum.62), channel_id=1, replica_groups=mesh['batch'=16,'patch'=16] {'patch'}, use_global_device_ids=true, to_apply=%region_5.6 | all-reduce | flops 32 | bytes 256 | tf_op jit(solution)/shard_map/psum | solution.py:23
  96.5 119.0 %all-gather.7.cloned.1.call-done = bf16[32,64,1280]{2,1,0:T(8,128)(2,1)} async-done(((bf16[2,64,1280]{2,1,0:T(8,128)(2,1)}), bf16[32,64,1280]{2,1,0:T(8,128)(2,1)}) %all-gather.7.cloned.1.call-update) | async-done | bytes 5242896 | tf_op jit(solution)/shard_map/all_gather | solution.py:67
  215.5 31.1 %pad_slice_fusion = (bf16[32,64,1280]{2,1,0:T(8,128)(2,1)S(1)}, bf16[32,64,1280]{2,1,0:T(8,128)(2,1)}, bf16[32,64,1280]{2,1,0:T(8,128)(2,1)}, bf16[32,64,1280]{2...) fusion(bf16[32,64,1280]{2,1,0:T(8,128)(2,1)} %all-gather.7.clon, ...), kind=kLoop, calls=%fused_computation.16 | loop fusion | bytes 47185920 | tf_op jit(solution)/shard_map/slice | solution.py:32
  246.7 4.4 fusion.37
  266.3 33.3 %all_to_all.14 = bf16[32,64,80]{2,1,0:T(8,128)(2,1)S(1)} all-to-all(bf16[32,64,80]{2,1,0:T(8,128)(2,1)S(1)} %bitcast.135), channel_id=1, replica_groups=mesh['batch'=16,'patch'=16] {'patch'}, dimensions={0} | all-to-all | bytes 655360 | tf_op jit(solution)/shard_map/all_to_all | solution.py:72
  300.8 38.9 %psum.30 = f32[32]{0:T(128)S(1)} all-reduce(f32[32]{0:T(128)S(1)} %reduce_sum.81), channel_id=1, replica_groups=mesh['batch'=16,'patch'=16] {'patch'}, use_global_device_ids=true, to_apply=%region_8.9 | all-reduce | flops 32 | bytes 256 | tf_op jit(solution)/shard_map/psum | solution.py:21
  340.2 39.7 %psum.31 = f32[32]{0:T(128)S(1)} all-reduce(f32[32]{0:T(128)S(1)} %reduce_sum.84), channel_id=1, replica_groups=mesh['batch'=16,'patch'=16] {'patch'}, use_global_device_ids=true, to_apply=%region_11.12 | all-reduce | flops 32 | bytes 256 | tf_op jit(solution)/shard_map/psum | solution.py:23
  380.1 4.0 convolution_convert_fusion.1
  384.2 24.5 %all-gather.15.cloned.1.call-done = bf16[1280,1280]{1,0:T(8,128)(2,1)} async-done(((bf16[80,1280]{1,0:T(8,128)(2,1)}), bf16[1280,1280]{1,0:T(8,128)(2,1)}) %all-gather.15.cloned.1.call-update) | async-done | bytes 3276816 | tf_op jit(solution)/shard_map/all_gather | solution.py:82
  408.7 3.9 convolution_convert_fusion
  414.5 4.3 all-to-all-start.1
  418.9 130.7 %all-gather.9.cloned.1.call-done = bf16[1280,1280]{1,0:T(8,128)(2,1)} async-done(((bf16[80,1280]{1,0:T(8,128)(2,1)}), bf16[1280,1280]{1,0:T(8,128)(2,1)}) %all-gather.9.cloned.1.call-update) | async-done | bytes 3276816 | tf_op jit(solution)/shard_map/all_gather | solution.py:80
  549.6 4.0 convolution_convert_fusion.2
  555.5 117.1 %all-gather.13.cloned.1.call-done = bf16[2048,1280]{1,0:T(8,128)(2,1)} async-done(((bf16[128,1280]{1,0:T(8,128)(2,1)}), bf16[2048,1280]{1,0:T(8,128)(2,1)}) %all-gather.13.cloned.1.call-update) | async-done | bytes 5242896 | tf_op jit(solution)/shard_map/all_gather | solution.py:88
  672.6 7.9 copy.30
  680.5 114.0 %all-gather.17.cloned.1.call-done = bf16[2048,1280]{1,0:T(8,128)(2,1)} async-done(((bf16[128,1280]{1,0:T(8,128)(2,1)}), bf16[2048,1280]{1,0:T(8,128)(2,1)}) %all-gather.17.cloned.1.call-update) | async-done | bytes 5242896 | tf_op jit(solution)/shard_map/all_gather | solution.py:89
  794.5 8.0 copy.31
  802.5 72.1 %while.10 = (s32[]{:T(128)}, bf16[20,128,64]{1,2,0:T(8,128)(2,1)}, bf16[20,128,64]{1,2,0:T(8,128)(2,1)}, bf16[20,2048,64]{1,2,0:T(8,128)(2,1)}, bf16[20,2048,64]{1,2,0:T(8,128)(2,1)}, /*index=5*/s32[]{:T(128)}) while((s32[]{:T(128)}, bf16[20,128,64]{1,2,0:T(8,128)(2,1)}, bf16[20,128,64]{1,2,0:T(8,128)(2,1)}, ...), condition=%wide.region_15.16_spmd, body=%wide.region_12.15_spmd.sunk | while | flops 68689664 | bytes 3723845 | solution.py:57
  804.2 1.9 fusion.75
  807.8 1.9 fusion.75
  811.4 1.9 fusion.75
  818.6 1.9 fusion.75
  825.8 1.9 fusion.75
  833.0 1.9 fusion.75
  836.6 1.9 fusion.75
  843.8 1.9 fusion.75
  847.4 1.9 fusion.75
  858.2 1.9 fusion.75
  861.8 1.9 fusion.75
  872.7 1.9 fusion.75
  874.6 3.0 fusion.14
  (144 shorter events, 76.4 us)
Async XLA Ops:
  6.5 209.0 %all-gather.7.cloned.1.call-start = ((), (), s32[]{:S(2)}) async-start(), calls=%async_computation.2 | async-start | bytes 5570560 | tf_op jit(solution)/shard_map/all_gather | solution.py:67
  94.4 285.8 %all-gather.11.cloned.1.call-start = ((), (), s32[]{:S(2)}) async-start(), calls=%async_computation.4 | async-start | bytes 3481600 | tf_op jit(solution)/shard_map/all_gather | solution.py:81
  95.1 313.6 %all-gather.15.cloned.1.call-start = ((), (), s32[]{:S(2)}) async-start(), calls=%async_computation.6 | async-start | bytes 3481600 | tf_op jit(solution)/shard_map/all_gather | solution.py:82
  95.8 453.8 %all-gather.9.cloned.1.call-start = ((), (), s32[]{:S(2)}) async-start(), calls=%async_computation.3 | async-start | bytes 3481600 | tf_op jit(solution)/shard_map/all_gather | solution.py:80
  96.4 150.2 %copy-start.5 = (bf16[3,3,80,1280]{3,2,1,0:T(8,128)(2,1)S(1)}, bf16[3,3,80,1280]{3,2,1,0:T(8,128)(2,1)}, u32[]{:S(2)}) copy-start(bf16[3,3,80,1280]{3,2,1,0:T(8,128)(2,1)} %param.10) | copy-start | bytes 5529604
  96.4 576.1 %all-gather.13.cloned.1.call-start = ((), (), s32[]{:S(2)}) async-start(), calls=%async_computation.5 | async-start | bytes 5570560 | tf_op jit(solution)/shard_map/all_gather | solution.py:88
  246.6 4.4 copy-start.1
  246.7 8.6 slice-start.8
  251.0 2.5 copy-start
  251.0 4.2 slice-start.9
  253.5 3.4 slice-start
  253.5 5.6 slice-start.6
  255.2 2.2 slice-start.1
  255.3 3.9 slice-start.7
  257.0 3.9 slice-start.4
  259.1 1.8 slice-start.5
  259.2 3.5 slice-start.2
  260.9 1.7 slice-start.3
  262.6 1.7 copy-start.7
  264.3 36.1 %copy-start.3 = (bf16[2,64,1280]{2,1,0:T(8,128)(2,1)S(1)}, bf16[2,64,1280]{2,1,0:T(8,128)(2,1)}, u32[]{:S(2)}) copy-start(bf16[2,64,1280]{2,1,0:T(8,128)(2,1)} %param.9) | copy-start | bytes 983044
  300.5 114.0 %copy-start.2 = (bf16[2,64,1280]{2,1,0:T(8,128)(2,1)}, bf16[2,64,1280]{2,1,0:T(8,128)(2,1)S(1)}, u32[]{:S(2)}) copy-start(bf16[2,64,1280]{2,1,0:T(8,128)(2,1)S(1)} %fusion.26) | copy-start | bytes 983044
  300.6 112.1 %copy-start.6 = (bf16[80,1280]{1,0:T(8,128)(2,1)S(1)}, bf16[80,1280]{1,0:T(8,128)(2,1)}, u32[]{:S(2)}) copy-start(bf16[80,1280]{1,0:T(8,128)(2,1)} %param.15) | copy-start | bytes 614404
  380.1 34.4 %copy-start.4 = (bf16[128,1280]{1,0:T(8,128)(2,1)}, bf16[128,1280]{1,0:T(8,128)(2,1)S(1)}, u32[]{:S(2)}) copy-start(bf16[128,1280]{1,0:T(8,128)(2,1)S(1)} %fusion.28) | copy-start | bytes 983044
  384.1 410.4 %all-gather.17.cloned.1.call-start = ((), (), s32[]{:S(2)}) async-start(), calls=%async_computation.7 | async-start | bytes 5570560 | tf_op jit(solution)/shard_map/all_gather | solution.py:89
  414.5 460.1 %all-to-all-start.1 = ((bf16[16,80,1280]{2,1,0:T(8,128)(2,1)}), bf16[16,80,1280]{2,1,0:T(8,128)(2,1)S(1)}, u32[]{:S(2)}, u32[]{:S(2)}) async-start(bf16[16,80,1280]{2,1,0:T(8,128)(2,1)} %stack.2), calls=%async_computation.1 | async-start | bytes 6553600 | tf_op jit(solution)/shard_map/all_to_all | solution.py:95
Sparse Core Ops, SparseCore 0:
  94.5 120.9 all-gather.6
  217.3 97.4 all-gather.10
  316.6 92.0 all-gather.14
  410.4 139.2 all-gather.8
  551.3 121.2 all-gather.12
  674.2 120.2 all-gather.16
